TPU v7x, 32 devices: a whole 2x2x4 slice. The times are simulated.
32 devices in a mesh: frames: 8 (over z, core), heads: 4 (over y, x).
Axes of the slice: x: 2, y: 2, z: 4, core: 2. Of those that a mesh axis runs over, the one named last changes fastest.
Arguments:
- clip: bfloat16 [16, 8, 128, 320], P('frames', 'heads'), may hold values from -6 to 6
- w_time: bfloat16 [3, 320, 320], replicated, may hold values from -0.1875 to 0.1875
- w_down: bfloat16 [320, 1280], replicated, may hold values from -0.3125 to 0.3125
- w_embed: bfloat16 [320, 1280], replicated, may hold values from -0.3125 to 0.3125
- w_qkv: bfloat16 [1280, 3840], P(None, 'heads'), may hold values from -0.15625 to 0.15625
- w_out: bfloat16 [1280, 1280], P('heads'), may hold values from -0.15625 to 0.15625
- w_up: bfloat16 [1280, 320], replicated, may hold values from -0.15625 to 0.15625
- timestep: int32 [1], replicated, may hold values from 0 to 999
- cotangent: bfloat16 [16, 8, 128, 320], P('frames', 'heads'), may hold values from -6 to 6
Outputs:
- output: bfloat16 [16, 8, 128, 320], P('frames', 'heads')
- grad_clip: float32 [16, 8, 128, 320], P('frames', 'heads')
- grad_time: float32 [3, 320, 320], replicated
- grad_down: float32 [320, 1280], replicated
- grad_embed: float32 [320, 1280], replicated
- grad_qkv: float32 [1280, 3840], P(None, 'heads')
- grad_out: float32 [1280, 1280], P('heads')
- grad_up: float32 [1280, 320], replicated
All inputs are finite; a program needn't handle non-finite values.
Results may differ from a plain program's by a relative error of at most 0.024.
Values may be sent and summed in bfloat16 or wider, within the bound.
No kernel may reach another device: no remote copies, remote signals or barrier semaphores. Data moves between devices by JAX's collectives and lax.ppermute only.
A program may use at most 128 MiB of HBM per device.

v0:
```python
import math
import jax
import jax.numpy as jnp
from jax import lax
from jax.sharding import PartitionSpec as P

HD = 80


def extended(cells, sides, width):
    for axis, dim in sides:
        count = lax.axis_size(axis)
        ends = count - 1
        head = lax.slice_in_dim(cells, 0, width, axis=dim)
        tail = lax.slice_in_dim(cells, cells.shape[dim] - width, cells.shape[dim], axis=dim)
        cells = jnp.concatenate(
            [
                lax.ppermute(tail, axis, [(i, (i + 1) % count) for i in range(ends)]),
                cells,
                lax.ppermute(head, axis, [((i + 1) % count, i) for i in range(ends)]),
            ],
            axis=dim,
        )
    return cells


def matmul(left, right):
    return jnp.dot(left, right, preferred_element_type=jnp.float32)


def inner_rows(left, right):
    return lax.dot_general(
        left, right, (((0,), (0,)), ((), ())), preferred_element_type=jnp.float32
    )


def inner_cols(left, right):
    return lax.dot_general(
        left, right, (((1,), (1,)), ((), ())), preferred_element_type=jnp.float32
    )


def upsample(field):
    return jnp.repeat(jnp.repeat(jnp.repeat(field, 2, 0), 2, 1), 2, 2)


def time_embed(timestep, width):
    half = width // 2
    freqs = jnp.exp(-math.log(10000.0) * jnp.arange(half, dtype=jnp.float32) / half)
    angle = timestep.astype(jnp.float32)[0] * freqs
    return jax.nn.silu(jnp.concatenate([jnp.cos(angle), jnp.sin(angle)])).astype(jnp.bfloat16)


def to_coarse(field):
    local = lax.all_to_all(field, "frames", split_axis=2, concat_axis=0, tiled=True)
    whole = lax.all_gather(local, "heads", axis=1, tiled=True)
    return (local, whole)


def coarse_sum(partial_value):
    return lax.psum_scatter(
        partial_value.astype(jnp.bfloat16), "heads", scatter_dimension=1, tiled=True
    ).astype(jnp.float32)


def to_fine(field):
    return lax.all_to_all(field, "frames", split_axis=0, concat_axis=2, tiled=True)


def shards(clip, w_time, w_down, w_embed, w_qkv, w_out, w_up, timestep, cotangent):
    frames, rows, columns, chans = clip.shape
    width = w_down.shape[1]
    half_f, half_r, half_c = (frames // 2, rows // 2, columns // 2)
    scale = 1.0 / math.sqrt(HD)
    padded = extended(clip, (("frames", 0),), 1)
    branch = jnp.zeros((frames * rows * columns, chans), jnp.float32)
    for tap in range(3):
        branch = branch + matmul(padded[tap : tap + frames].reshape(-1, chans), w_time[tap])
    hidden = (clip.astype(jnp.float32).reshape(-1, chans) + branch).astype(jnp.bfloat16)
    hidden_f = hidden.astype(jnp.float32).reshape(frames, rows, columns, chans)
    pooled = hidden_f.reshape(half_f, 2, half_r, 2, half_c, 2, chans).mean(axis=(1, 3, 5))
    pooled = pooled.astype(jnp.bfloat16).reshape(-1, chans)
    embed = time_embed(timestep, w_embed.shape[0])
    shift = matmul(embed[None, :], w_embed)
    coarse_in = (matmul(pooled, w_down) + shift).astype(jnp.bfloat16)
    coarse_in = coarse_in.reshape(half_f, 1, half_r * half_c, width)
    local_in, full_in = to_coarse(coarse_in)
    coarse_frames, groups, per_group = (full_in.shape[0], full_in.shape[1], full_in.shape[2])
    places = groups * per_group
    token_mat = full_in.reshape(-1, width)
    heads_here = w_qkv.shape[1] // (3 * HD)
    qkv = (
        matmul(token_mat, w_qkv)
        .astype(jnp.bfloat16)
        .reshape(coarse_frames, places, heads_here, 3, HD)
    )
    query = qkv[:, :, :, 0]
    keys = qkv[:, :, :, 1]
    values = qkv[:, :, :, 2]
    scores = jnp.einsum("tpnd,spnd->ntsp", query, keys, preferred_element_type=jnp.float32) * scale
    probs = jax.nn.softmax(scores, axis=2)
    weights = probs.astype(jnp.bfloat16)
    attended = jnp.einsum("ntsp,spnd->tpnd", weights, values, preferred_element_type=jnp.float32)
    attended = attended.astype(jnp.bfloat16).reshape(-1, heads_here * HD)
    mixed = coarse_sum(matmul(attended, w_out).reshape(coarse_frames, groups, per_group, width))
    coarse_out = (local_in.astype(jnp.float32) + mixed).astype(jnp.bfloat16)
    fine_back = to_fine(coarse_out).reshape(-1, width)
    lifted = matmul(fine_back, w_up).reshape(half_f, half_r, half_c, chans)
    output = (hidden_f + upsample(lifted)).astype(jnp.bfloat16)
    upstream = cotangent.astype(jnp.float32)
    pooled_grad = upstream.reshape(half_f, 2, half_r, 2, half_c, 2, chans).sum(axis=(1, 3, 5))
    pooled_grad = pooled_grad.astype(jnp.bfloat16).reshape(-1, chans)
    grad_up_part = inner_rows(fine_back, pooled_grad)
    back_in = (
        inner_cols(pooled_grad, w_up)
        .astype(jnp.bfloat16)
        .reshape(half_f, 1, half_r * half_c, width)
    )
    local_grad, full_grad = to_coarse(back_in)
    grad_mat = full_grad.reshape(-1, width)
    grad_out_part = inner_rows(attended, grad_mat)
    attend_grad = inner_cols(grad_mat, w_out).astype(jnp.bfloat16)
    attend_grad = attend_grad.reshape(coarse_frames, places, heads_here, HD)
    weight_grad = jnp.einsum(
        "tpnd,spnd->ntsp", attend_grad, values, preferred_element_type=jnp.float32
    )
    score_grad = probs * (weight_grad - jnp.sum(probs * weight_grad, axis=2, keepdims=True)) * scale
    score_grad = score_grad.astype(jnp.bfloat16)
    query_grad = jnp.einsum("ntsp,spnd->tpnd", score_grad, keys, preferred_element_type=jnp.float32)
    keys_grad = jnp.einsum("ntsp,tpnd->spnd", score_grad, query, preferred_element_type=jnp.float32)
    values_grad = jnp.einsum(
        "ntsp,tpnd->spnd", weights, attend_grad, preferred_element_type=jnp.float32
    )
    qkv_grad = jnp.stack([query_grad, keys_grad, values_grad], axis=3).astype(jnp.bfloat16)
    qkv_grad = qkv_grad.reshape(-1, heads_here * 3 * HD)
    grad_qkv_part = inner_rows(token_mat, qkv_grad)
    input_grad = coarse_sum(
        inner_cols(qkv_grad, w_qkv).reshape(coarse_frames, groups, per_group, width)
    )
    coarse_grad = (input_grad + local_grad.astype(jnp.float32)).astype(jnp.bfloat16)
    fine_grad = to_fine(coarse_grad).reshape(-1, width)
    column_sum = jnp.sum(fine_grad.astype(jnp.float32), axis=0)
    grad_down_part = inner_rows(pooled, fine_grad)
    spread = inner_cols(fine_grad, w_down).reshape(half_f, half_r, half_c, chans)
    hidden_grad = (upstream + upsample(spread) * 0.125).astype(jnp.bfloat16)
    grad_padded = extended(hidden_grad, (("frames", 0),), 1)
    flat_grad = hidden_grad.reshape(-1, chans)
    grad_clip = flat_grad.astype(jnp.float32)
    taps = []
    for tap in range(3):
        grad_clip = grad_clip + inner_cols(
            grad_padded[2 - tap : 2 - tap + frames].reshape(-1, chans), w_time[tap]
        )
        taps.append(inner_rows(padded[tap : tap + frames].reshape(-1, chans), flat_grad))
    grad_clip = grad_clip.reshape(frames, rows, columns, chans)
    coarse_sums = (
        lax.psum(grad_qkv_part.astype(jnp.bfloat16), "frames").astype(jnp.float32),
        lax.psum(grad_out_part.astype(jnp.bfloat16), "frames").astype(jnp.float32),
    )
    fine_sums = lax.psum(
        (jnp.stack(taps), grad_down_part, grad_up_part, column_sum), ("frames", "heads")
    )
    grad_embed = embed.astype(jnp.float32)[:, None] * fine_sums[3][None, :]
    return (
        output,
        grad_clip,
        fine_sums[0],
        fine_sums[1],
        grad_embed,
        coarse_sums[0],
        coarse_sums[1],
        fine_sums[2],
    )


def solution(mesh):
    return jax.shard_map(
        shards,
        mesh=mesh,
        in_specs=(
            P("frames", "heads", None, None),
            P(),
            P(),
            P(),
            P(None, "heads"),
            P("heads", None),
            P(),
            P(),
            P("frames", "heads", None, None),
        ),
        out_specs=(
            P("frames", "heads", None, None),
            P("frames", "heads", None, None),
            P(),
            P(),
            P(),
            P(None, "heads"),
            P("heads", None),
            P(),
        ),
        check_vma=False,
    )
```

profile of v0, /device:TPU:0, one launch (start us, length us, event | category | flops | bytes accessed | tf_op | source)
XLA Modules:
  0.0 432.7 jit_solution(15819610578393598799)
XLA Ops:
  9.1 3.1 collective-permute-start
  20.1 7.6 %all-to-all-start.2 = ((bf16[8,2,5120]{2,1,0:T(2,128)(2,1)}), bf16[8,2,5120]{2,1,0:T(2,128)(2,1)}, u32[]{:S(2)}, u32[]{:S(2)}) async-start(bf16[8,2,5120]{2,1,0:T(2,128)(2,1)} %reshape.238), calls=%async_computation.2 | async-start | bytes 327680 | tf_op jit(solution)/shard_map/all_to_all | solution.py:55
  45.7 2.5 reshape_reshape.3
  53.8 5.1 %all-to-all-start = ((bf16[8,2,5120]{2,1,0:T(2,128)(2,1)}), bf16[8,2,5120]{2,1,0:T(2,128)(2,1)}, u32[]{:S(2)}, u32[]{:S(2)}) async-start(bf16[8,2,5120]{2,1,0:T(2,128)(2,1)} %reshape.236), calls=%async_computation | async-start | bytes 327680 | tf_op jit(solution)/shard_map/all_to_all | solution.py:55
  62.1 11.6 %all_gather.7 = bf16[8,4,8,1280]{3,2,0,1:T(8,128)(2,1)S(1)} all-gather(bf16[8,1,8,1280]{3,2,0,1:T(8,128)(2,1)S(1)} %bitcast.199), channel_id=1, replica_groups=mesh['frames'=8,'heads'=4] {'heads'}, dimensions={1}, use_global_device_ids=true | all-gather | bytes 819200 | tf_op jit(solution)/shard_map/all_gather | solution.py:56
  77.6 11.5 %all_gather.6 = bf16[8,4,8,1280]{3,2,0,1:T(8,128)(2,1)S(1)} all-gather(bf16[8,1,8,1280]{3,2,0,1:T(8,128)(2,1)S(1)} %bitcast.200), channel_id=1, replica_groups=mesh['frames'=8,'heads'=4] {'heads'}, dimensions={1}, use_global_device_ids=true | all-gather | bytes 819200 | tf_op jit(solution)/shard_map/all_gather | solution.py:56
  91.8 3.3 reshape.210
  101.2 2.2 fusion.9
  108.4 2.2 convolution_bitcast_fusion.1
  113.8 2.3 convolution_convert_fusion.3
  118.6 2.7 convolution_convert_fusion.2
  126.0 2.3 convolution_convert_fusion
  128.3 49.5 %all-reduce.13.cloned.1.call-done = (bf16[8,4,8,1280]{3,2,1,0:T(8,128)(2,1)}, bf16[8,4,8,1280]{3,2,1,0:T(8,128)(2,1)}) async-done(((bf16[8,4,8,1280]{3,2,1,0:T(8,128)(2,1)}, bf16[8,4,8,1280]{3,2,1,0:T(8,128)(2,1)}), (bf16[8,4,8,1280]{3,2,1,0:T(8,128)(2,1)}, bf16[8,4,8,1280]{3,2,1,0:T(8,128)(2,1)})) %all-reduce.13.cloned.1.call-update) | async-done | bytes 1310736
  177.8 2.3 fusion.43
  180.1 4.6 %all-to-all-start.3 = ((bf16[8,1,8,1280]{3,2,1,0:T(8,128)(2,1)}), bf16[8,1,8,1280]{3,2,1,0:T(8,128)(2,1)S(1)}, u32[]{:S(2)}, u32[]{:S(2)}) async-start(bf16[8,1,8,1280]{3,2,1,0:T(8,128)(2,1)} %fusion.43), calls=%async_computation.3 | async-start | bytes 327680 | tf_op jit(solution)/shard_map/all_to_all | solution.py:67
  184.7 2.4 fusion.42
  187.1 6.5 %all-to-all-done.3 = bf16[8,1,8,1280]{3,2,1,0:T(8,128)(2,1)S(1)} async-done(((bf16[8,1,8,1280]{3,2,1,0:T(8,128)(2,1)}), bf16[8,1,8,1280]{3,2,1,0:T(8,128)(2,1)S(1)}, u32[]{:S(2)}, u32[]{:S(2)}) %all-to-all-start.3) | async-done | bytes 163872 | tf_op jit(solution)/shard_map/all_to_all | solution.py:67
  193.5 3.4 all-to-all-start.1
  200.6 5.6 %all-to-all-done.1 = bf16[8,1,8,1280]{3,2,1,0:T(8,128)(2,1)S(1)} async-done(((bf16[8,1,8,1280]{3,2,1,0:T(8,128)(2,1)}), bf16[8,1,8,1280]{3,2,1,0:T(8,128)(2,1)S(1)}, u32[]{:S(2)}, u32[]{:S(2)}) %all-to-all-start.1) | async-done | bytes 163872 | tf_op jit(solution)/shard_map/all_to_all | solution.py:67
  214.0 43.6 %psum.44 = f32[1280]{0:T(1024)S(1)} all-reduce(f32[1280]{0:T(1024)S(1)} %convert_reduce_fusion.1), channel_id=1, replica_groups=mesh['frames'=8,'heads'=4] {'frames','heads'}, use_global_device_ids=true, to_apply=%region_11.12 | all-reduce | flops 1280 | bytes 10240 | tf_op jit(solution)/shard_map/psum | solution.py:160
  259.8 7.7 %all-reduce.11.cloned.1.call-done = (bf16[1280,960]{0,1:T(8,128)(2,1)}, bf16[320,1280]{1,0:T(8,128)(2,1)}) async-done(((bf16[1280,960]{0,1:T(8,128)(2,1)}, bf16[320,1280]{1,0:T(8,128)(2,1)}), (bf16[1280,960]{0,1:T(8,128)(2,1)}, bf16[320,1280]{1,0:T(8,128)(2,1)})) %all-reduce.11.cloned.1.call-update) | async-done | bytes 3276816 | tf_op jit(solution)/shard_map/psum | solution.py:157
  267.4 4.4 %convert_element_type.187 = f32[1280,960]{0,1:T(8,128)} convert(bf16[1280,960]{0,1:T(8,128)(2,1)} %get-tuple-element.59) | non-fusion elementwise | flops 1228800 | bytes 7372800 | tf_op jit(solution)/shard_map/convert_element_type | solution.py:157
  276.5 143.7 %all-reduce.9.cloned.1.call-done = (f32[3,320,320]{2,1,0:T(8,128)}, f32[320,1280]{1,0:T(8,128)}, f32[1280,320]{0,1:T(8,128)}) async-done(((f32[3,320,320]{2,1,0:T(8,128)}, f32[320,1280]{1,0:T(8,128)}, f32[1280,320]{0,1:T(8,128)}), (f32[3,320,320]{2,1,0:T(8,128)}, f32[320,1280]{1,0:T(8,128)}, f32[1280,320]{0,1:T(8,128)})) %all-reduce.9.cloned.1.call-update) | async-done | bytes 4505616 | tf_op jit(solution)/shard_map/psum | solution.py:160
  420.3 2.7 copy.287
  (204 shorter events, 84.8 us)
Async XLA Ops:
  7.2 82.8 %copy-start = (bf16[1280,960]{0,1:T(8,128)(2,1)S(1)}, bf16[1280,960]{0,1:T(8,128)(2,1)}, u32[]{:S(2)}) copy-start(bf16[1280,960]{0,1:T(8,128)(2,1)} %param.13) | copy-start | bytes 7372804
  9.1 21.3 %collective-permute-start = (bf16[1,2,128,320]{2,3,1,0:T(8,128)(2,1)}, bf16[1,2,128,320]{2,3,1,0:T(8,128)(2,1)}, u32[]{:S(2)}, u32[]{:S(2)}) collective-permute-start(bf16[1,2,128,320]{2,3,1,0:T(8,128)(2,1)} %get-tuple-element.73), channel_id=1, source_target_pairs={{0,4},{4,8},{8,12},{12,16},{16,20},{20,24},{24,28},{1,5},{5,9},{9,... | collective-permute-start | bytes 491528 | tf_op jit(solution)/shard_map/ppermute | solution.py:18
  12.1 23.8 %collective-permute-start.1 = (bf16[1,2,128,320]{2,3,1,0:T(8,128)(2,1)}, bf16[1,2,128,320]{2,3,1,0:T(8,128)(2,1)}, u32[]{:S(2)}, u32[]{:S(2)}) collective-permute-start(bf16[1,2,128,320]{2,3,1,0:T(8,128)(2,1)} %get-tuple-element.72), channel_id=1, source_target_pairs={{4,0},{8,4},{12,8},{16,12},{20,16},{24,20},{28,24},{5,1},{9,5},{13... | collective-permute-start | bytes 491528 | tf_op jit(solution)/shard_map/ppermute | solution.py:20
  14.6 13.9 %copy-start.6 = (bf16[2,2,128,320]{2,3,1,0:T(8,128)(2,1)S(1)}, bf16[2,2,128,320]{2,3,1,0:T(8,128)(2,1)}, u32[]{:S(2)}) copy-start(bf16[2,2,128,320]{2,3,1,0:T(8,128)(2,1)} %param.9) | copy-start | bytes 983044
  20.1 33.7 %all-to-all-start.2 = ((bf16[8,2,5120]{2,1,0:T(2,128)(2,1)}), bf16[8,2,5120]{2,1,0:T(2,128)(2,1)}, u32[]{:S(2)}, u32[]{:S(2)}) async-start(bf16[8,2,5120]{2,1,0:T(2,128)(2,1)} %reshape.238), calls=%async_computation.2 | async-start | bytes 327680 | tf_op jit(solution)/shard_map/all_to_all | solution.py:55
  34.0 7.4 %copy-start.12 = (bf16[3,320,320]{2,1,0:T(8,128)(2,1)S(1)}, bf16[3,320,320]{2,1,0:T(8,128)(2,1)}, u32[]{:S(2)}) copy-start(bf16[3,320,320]{2,1,0:T(8,128)(2,1)} %param.10) | copy-start | bytes 1843204
  53.8 22.3 %all-to-all-start = ((bf16[8,2,5120]{2,1,0:T(2,128)(2,1)}), bf16[8,2,5120]{2,1,0:T(2,128)(2,1)}, u32[]{:S(2)}, u32[]{:S(2)}) async-start(bf16[8,2,5120]{2,1,0:T(2,128)(2,1)} %reshape.236), calls=%async_computation | async-start | bytes 327680 | tf_op jit(solution)/shard_map/all_to_all | solution.py:55
  58.9 15.7 %copy-start.8 = (bf16[320,1280]{1,0:T(8,128)(2,1)S(1)}, bf16[320,1280]{1,0:T(8,128)(2,1)}, u32[]{:S(2)}) copy-start(bf16[320,1280]{1,0:T(8,128)(2,1)} %param.14) | copy-start | bytes 2457604
  58.9 118.9 %all-reduce.13.cloned.1.call-start = ((), (), s32[]{:S(2)}) async-start(), calls=%async_computation.6 | async-start | bytes 2621440
  77.5 13.3 %copy-start.15 = (bf16[64,1,1,1280]{3,2,1,0:T(2,128)(2,1)}, bf16[64,1,1,1280]{3,2,1,0:T(2,128)(2,1)S(1)}, u32[]{:S(2)}) copy-start(bf16[64,1,1,1280]{3,2,1,0:T(2,128)(2,1)S(1)} %reshape.237) | copy-start | bytes 491524
  98.1 5.3 %copy-start.22 = (bf16[8,32,4,80]{3,2,1,0:T(4,128)(2,1)S(1)}, bf16[8,32,4,80]{3,2,1,0:T(4,128)(2,1)}, u32[]{:S(2)}) copy-start(bf16[8,32,4,80]{3,2,1,0:T(4,128)(2,1)} %reshape.214) | copy-start | bytes 491524
  107.0 6.8 %copy-start.9 = (bf16[320,1280]{1,0:T(8,128)(2,1)S(1)}, bf16[320,1280]{1,0:T(8,128)(2,1)}, u32[]{:S(2)}) copy-start(bf16[320,1280]{1,0:T(8,128)(2,1)} %param.14) | copy-start | bytes 2457604
  121.4 146.0 %all-reduce.11.cloned.1.call-start = ((), (), s32[]{:S(2)}) async-start(), calls=%async_computation.5 | async-start | bytes 6553600 | tf_op jit(solution)/shard_map/psum | solution.py:157
  128.3 49.5 %copy-start.14 = (bf16[64,1,1,1280]{3,2,1,0:T(2,128)(2,1)S(1)}, bf16[64,1,1,1280]{3,2,1,0:T(2,128)(2,1)}, u32[]{:S(2)}) copy-start(bf16[64,1,1,1280]{3,2,1,0:T(2,128)(2,1)} %reshape.239) | copy-start | bytes 491524
  128.3 56.4 %copy-start.16 = (bf16[64,1,1,1280]{3,2,1,0:T(2,128)(2,1)S(1)}, bf16[64,1,1,1280]{3,2,1,0:T(2,128)(2,1)}, u32[]{:S(2)}) copy-start(bf16[64,1,1,1280]{3,2,1,0:T(2,128)(2,1)} %copy-done.15) | copy-start | bytes 491524
  128.3 68.7 %copy-start.10 = (bf16[320,1280]{1,0:T(8,128)(2,1)S(1)}, bf16[320,1280]{1,0:T(8,128)(2,1)}, u32[]{:S(2)}) copy-start(bf16[320,1280]{1,0:T(8,128)(2,1)} %param.11) | copy-start | bytes 2457604
  180.1 13.5 %all-to-all-start.3 = ((bf16[8,1,8,1280]{3,2,1,0:T(8,128)(2,1)}), bf16[8,1,8,1280]{3,2,1,0:T(8,128)(2,1)S(1)}, u32[]{:S(2)}, u32[]{:S(2)}) async-start(bf16[8,1,8,1280]{3,2,1,0:T(8,128)(2,1)} %fusion.43), calls=%async_computation.3 | async-start | bytes 327680 | tf_op jit(solution)/shard_map/all_to_all | solution.py:67
  184.7 13.0 %copy-start.31 = (bf16[2,2,128,320]{2,3,1,0:T(8,128)(2,1)S(1)}, bf16[2,2,128,320]{2,3,1,0:T(8,128)(2,1)}, u32[]{:S(2)}) copy-start(bf16[2,2,128,320]{2,3,1,0:T(8,128)(2,1)} %param.17) | copy-start | bytes 983044
  193.5 12.7 %all-to-all-start.1 = ((bf16[8,1,8,1280]{3,2,1,0:T(8,128)(2,1)}), bf16[8,1,8,1280]{3,2,1,0:T(8,128)(2,1)S(1)}, u32[]{:S(2)}, u32[]{:S(2)}) async-start(bf16[8,1,8,1280]{3,2,1,0:T(8,128)(2,1)} %fusion.42), calls=%async_computation.1 | async-start | bytes 327680 | tf_op jit(solution)/shard_map/all_to_all | solution.py:67
  196.9 223.4 %all-reduce.9.cloned.1.call-start = ((), (), s32[]{:S(2)}) async-start(), calls=%async_computation.4 | async-start | bytes 9502720 | tf_op jit(solution)/shard_map/psum | solution.py:160
  199.4 6.9 %copy-start.41 = (bf16[64,320]{1,0:T(8,128)(2,1)S(1)}, bf16[64,320]{1,0:T(8,128)(2,1)}, u32[]{:S(2)}) copy-start(bf16[64,320]{1,0:T(8,128)(2,1)} %copy-done.40) | copy-start | bytes 122884
  200.6 7.2 %copy-start.38 = (f32[64,320]{1,0:T(8,128)S(1)}, f32[64,320]{1,0:T(8,128)}, u32[]{:S(2)}) copy-start(f32[64,320]{1,0:T(8,128)} %copy-done.37) | copy-start | bytes 245764
  211.3 61.8 %collective-permute-start.3 = (bf16[1,2,128,320]{2,3,1,0:T(8,128)(2,1)S(1)}, bf16[1,2,128,320]{2,3,1,0:T(8,128)(2,1)S(1)}, u32[]{:S(2)}, u32[]{:S(2)}) collective-permute-start(bf16[1,2,128,320]{2,3,1,0:T(8,128)(2,1)S(1)} %get-tuple-element.70), channel_id=1, source_target_pairs={{0,4},{4,8},{8,12},{12,16},{16,20},{20,24},{24,28},{1,5},{5,9},{9,... | collective-permute-start | bytes 491528 | tf_op jit(solution)/shard_map/ppermute | solution.py:18
  212.6 60.5 %collective-permute-start.2 = (bf16[1,2,128,320]{2,3,1,0:T(8,128)(2,1)S(1)}, bf16[1,2,128,320]{2,3,1,0:T(8,128)(2,1)S(1)}, u32[]{:S(2)}, u32[]{:S(2)}) collective-permute-start(bf16[1,2,128,320]{2,3,1,0:T(8,128)(2,1)S(1)} %get-tuple-element.71), channel_id=1, source_target_pairs={{4,0},{8,4},{12,8},{16,12},{20,16},{24,20},{28,24},{5,1},{9,5},{13... | collective-permute-start | bytes 491528 | tf_op jit(solution)/shard_map/ppermute | solution.py:20
  (31 other events, 66.6 us)
Sparse Core Ops, SparseCore 0:
  121.5 56.2 all-reduce.12
  180.8 86.5 all-reduce.10
  274.1 146.1 all-reduce.8
where the time goes:
time: 434 us; the launch traced here: 433 us
  waiting for transfers between devices  213 us (49%)
  blocking collectives  66.7 us (15%)
  local copies, waits for them, and re-layouts  55 us (13%)
  matrix products  32.1 us (7%)
  starting transfers between devices  27.9 us (6%)
  other arithmetic  22.9 us (5%)
  between operations  15.2 us (4%)
    psum x1, waiting for transfers between devices, shards(): lax.psum((jnp.stack(taps), grad_down_part, grad_up_part, column_sum), ('f...  144 us
    unnamed x4, waiting for transfers between devices  49.5 us
    psum x1, blocking collectives, shards(): lax.psum((jnp.stack(taps), grad_down_part, grad_up_part, column_sum), ('f...  43.6 us
    all_gather x2, blocking collectives, to_coarse(): whole = lax.all_gather(local, 'heads', axis=1, tiled=True)  23.1 us
    unnamed x103, local copies, waits for them, and re-layouts  22.5 us
    all_to_all x2, starting transfers between devices, to_coarse(): lax.all_to_all(field, 'frames', split_axis=2, concat_axis=0, tiled=True)  12.7 us
    all_to_all x2, waiting for transfers between devices, to_fine(): lax.all_to_all(field, 'frames', split_axis=0, concat_axis=2, tiled=True)  12.1 us
    dot_general x8, matrix products, matmul(): return jnp.dot(left, right, preferred_element_type=jnp.float32)  9.45 us
  transfers between devices with their start and end apart: 11, of which 5 were waited for; matrix products, arithmetic and copies ran while one was open for 15% of the time, Pallas kernels for 0%

commit v1 on v0

--- a/solution.py
+++ b/solution.py
@@ -157,8 +157,8 @@
         lax.psum(grad_qkv_part.astype(jnp.bfloat16), "frames").astype(jnp.float32),
         lax.psum(grad_out_part.astype(jnp.bfloat16), "frames").astype(jnp.float32),
     )
-    fine_sums = lax.psum(
-        (jnp.stack(taps), grad_down_part, grad_up_part, column_sum), ("frames", "heads")
+    fine_sums = jax.lax.psum(
+        jax.lax.psum((jnp.stack(taps), grad_down_part, grad_up_part, column_sum), "heads"), "frames"
     )
     grad_embed = embed.astype(jnp.float32)[:, None] * fine_sums[3][None, :]
     return (

time: 434 us -> 526 us (1.21)
  waiting for transfers between devices: 213 us -> 318 us
  blocking collectives: 66.7 us -> 49.8 us
    psum x1 -> x2, waiting for transfers between devices: 144 us -> 205 us  [the longest x1 104 us: shards(): jax.lax.psum((jnp.stack(taps), grad_down_part, grad_up_part, column_sum),...]
    psum x1, waiting for transfers between devices: 7.65 us -> 50.2 us  [shards(): lax.psum(grad_qkv_part.astype(jnp.bfloat16), 'frames').astype(jnp.float32)]
    psum x1 -> x2, blocking collectives: 43.6 us -> 26.8 us  [the longest x1 17.3 us: shards(): jax.lax.psum(jax.lax.psum((jnp.stack(taps), grad_down_part, grad_up_part,...]
    unnamed x4 -> x5, waiting for transfers between devices: 49.5 us -> 55.9 us
    unnamed x103 -> x101, local copies, waits for them, and re-layouts: 22.5 us -> 23.4 us
  transfers between devices with their start and end apart: 11 -> 12, of which waited for: 5 -> 6; matrix products, arithmetic and copies ran while one was open for 15% -> 12% of each run, Pallas kernels for 0% -> 0%
where the time goes in v1:
time: 526 us; the launch traced here: 525 us
  waiting for transfers between devices  318 us (60%)
  local copies, waits for them, and re-layouts  55.9 us (11%)
  blocking collectives  49.8 us (9%)
  matrix products  33.9 us (6%)
  starting transfers between devices  28.9 us (5%)
  other arithmetic  22.9 us (4%)
  between operations  15.2 us (3%)
    psum x1, waiting for transfers between devices, shards(): jax.lax.psum((jnp.stack(taps), grad_down_part, grad_up_part, column_sum),...  104 us
    psum x1, waiting for transfers between devices, shards(): jax.lax.psum(jax.lax.psum((jnp.stack(taps), grad_down_part, grad_up_part,...  101 us
    unnamed x5, waiting for transfers between devices  55.9 us
    psum x1, waiting for transfers between devices, shards(): lax.psum(grad_qkv_part.astype(jnp.bfloat16), 'frames').astype(jnp.float32)  50.2 us
    unnamed x101, local copies, waits for them, and re-layouts  23.4 us
    all_gather x2, blocking collectives, to_coarse(): whole = lax.all_gather(local, 'heads', axis=1, tiled=True)  23.1 us
    psum x1, blocking collectives, shards(): jax.lax.psum(jax.lax.psum((jnp.stack(taps), grad_down_part, grad_up_part,...  17.3 us
    all_to_all x2, starting transfers between devices, to_coarse(): lax.all_to_all(field, 'frames', split_axis=2, concat_axis=0, tiled=True)  12.7 us
  transfers between devices with their start and end apart: 12, of which 6 were waited for; matrix products, arithmetic and copies ran while one was open for 12% of the time, Pallas kernels for 0%

profile of v1, /device:TPU:0, one launch (start us, length us, event | category | flops | bytes accessed | tf_op | source)
XLA Modules:
  0.0 524.6 jit_solution(10677895231024471858)
XLA Ops:
  9.1 3.1 collective-permute-start
  20.1 7.6 %all-to-all-start.2 = ((bf16[8,2,5120]{2,1,0:T(2,128)(2,1)}), bf16[8,2,5120]{2,1,0:T(2,128)(2,1)}, u32[]{:S(2)}, u32[]{:S(2)}) async-start(bf16[8,2,5120]{2,1,0:T(2,128)(2,1)} %reshape.238), calls=%async_computation.2 | async-start | bytes 327680 | tf_op jit(solution)/shard_map/all_to_all | solution.py:55
  45.7 2.5 reshape_reshape.3
  53.8 5.1 all-to-all-start
  62.1 11.6 %all_gather.7 = bf16[8,4,8,1280]{3,2,0,1:T(8,128)(2,1)S(1)} all-gather(bf16[8,1,8,1280]{3,2,0,1:T(8,128)(2,1)S(1)} %bitcast.199), channel_id=1, replica_groups=mesh['frames'=8,'heads'=4] {'heads'}, dimensions={1}, use_global_device_ids=true | all-gather | bytes 819200 | tf_op jit(solution)/shard_map/all_gather | solution.py:56
  77.6 11.5 %all_gather.6 = bf16[8,4,8,1280]{3,2,0,1:T(8,128)(2,1)S(1)} all-gather(bf16[8,1,8,1280]{3,2,0,1:T(8,128)(2,1)S(1)} %bitcast.200), channel_id=1, replica_groups=mesh['frames'=8,'heads'=4] {'heads'}, dimensions={1}, use_global_device_ids=true | all-gather | bytes 819200 | tf_op jit(solution)/shard_map/all_gather | solution.py:56
  91.8 3.3 reshape.210
  113.8 2.3 convolution_convert_fusion.3
  118.6 2.7 convolution_convert_fusion.2
  122.0 55.8 %all-reduce.17.cloned.1.call-done = (bf16[8,4,8,1280]{3,2,1,0:T(8,128)(2,1)}, bf16[8,4,8,1280]{3,2,1,0:T(8,128)(2,1)}) async-done(((bf16[8,4,8,1280]{3,2,1,0:T(8,128)(2,1)}, bf16[8,4,8,1280]{3,2,1,0:T(8,128)(2,1)}), (bf16[8,4,8,1280]{3,2,1,0:T(8,128)(2,1)}, bf16[8,4,8,1280]{3,2,1,0:T(8,128)(2,1)})) %all-reduce.17.cloned.1.call-update) | async-done | bytes 1310736
  177.8 2.4 fusion.43
  180.2 4.6 all-to-all-start.3
  184.8 2.3 fusion.42
  187.1 4.9 all-to-all-done.3
  192.0 4.0 all-to-all-start.1
  203.2 2.5 fusion.47
  208.9 2.3 convolution_convert_fusion
  213.0 104.2 %all-reduce.13.cloned.1.call-done = (f32[3,320,320]{2,1,0:T(8,128)}, f32[320,1280]{1,0:T(8,128)}, f32[1280,320]{0,1:T(8,128)}) async-done(((f32[3,320,320]{2,1,0:T(8,128)}, f32[320,1280]{1,0:T(8,128)}, f32[1280,320]{0,1:T(8,128)}), (f32[3,320,320]{2,1,0:T(8,128)}, f32[320,1280]{1,0:T(8,128)}, f32[1280,320]{0,1:T(8,128)})) %all-reduce.13.cloned.1.call-update) | async-done | bytes 4505616 | tf_op jit(solution)/shard_map/psum | solution.py:161
  323.1 9.4 %psum.74 = f32[1280]{0:T(1024)S(1)} all-reduce(f32[1280]{0:T(1024)S(1)} %convert_reduce_fusion.1), channel_id=1, replica_groups=mesh['frames'=8,'heads'=4] {'heads'}, use_global_device_ids=true, to_apply=%region_13.14 | all-reduce | flops 1280 | bytes 10240 | tf_op jit(solution)/shard_map/psum | solution.py:161
  332.5 17.3 %psum.75 = f32[1280]{0:T(1024)S(1)} all-reduce(f32[1280]{0:T(1024)S(1)} %psum.74), channel_id=1, replica_groups=mesh['frames'=8,'heads'=4] {'frames'}, use_global_device_ids=true, to_apply=%region_14.15 | all-reduce | flops 1280 | bytes 10240 | tf_op jit(solution)/shard_map/psum | solution.py:160
  352.0 50.2 %all-reduce.15.cloned.1.call-done = (bf16[1280,960]{0,1:T(8,128)(2,1)}, bf16[320,1280]{1,0:T(8,128)(2,1)}) async-done(((bf16[1280,960]{0,1:T(8,128)(2,1)}, bf16[320,1280]{1,0:T(8,128)(2,1)}), (bf16[1280,960]{0,1:T(8,128)(2,1)}, bf16[320,1280]{1,0:T(8,128)(2,1)})) %all-reduce.15.cloned.1.call-update) | async-done | bytes 3276816 | tf_op jit(solution)/shard_map/psum | solution.py:157
  402.2 4.4 convert_element_type.187
  411.4 100.8 %all-reduce.11.cloned.1.call-done = (f32[3,320,320]{2,1,0:T(8,128)}, f32[320,1280]{1,0:T(8,128)}, f32[1280,320]{0,1:T(8,128)}) async-done(((f32[3,320,320]{2,1,0:T(8,128)}, f32[320,1280]{1,0:T(8,128)}, f32[1280,320]{0,1:T(8,128)}), (f32[3,320,320]{2,1,0:T(8,128)}, f32[320,1280]{1,0:T(8,128)}, f32[1280,320]{0,1:T(8,128)})) %all-reduce.11.cloned.1.call-update) | async-done | bytes 4505616 | tf_op jit(solution)/shard_map/psum | solution.py:160
  512.2 2.7 copy.290
  (206 shorter events, 91.9 us)
Async XLA Ops:
  7.2 82.8 %copy-start = (bf16[1280,960]{0,1:T(8,128)(2,1)S(1)}, bf16[1280,960]{0,1:T(8,128)(2,1)}, u32[]{:S(2)}) copy-start(bf16[1280,960]{0,1:T(8,128)(2,1)} %param.13) | copy-start | bytes 7372804
  9.1 21.3 %collective-permute-start = (bf16[1,2,128,320]{2,3,1,0:T(8,128)(2,1)}, bf16[1,2,128,320]{2,3,1,0:T(8,128)(2,1)}, u32[]{:S(2)}, u32[]{:S(2)}) collective-permute-start(bf16[1,2,128,320]{2,3,1,0:T(8,128)(2,1)} %get-tuple-element.76), channel_id=1, source_target_pairs={{0,4},{4,8},{8,12},{12,16},{16,20},{20,24},{24,28},{1,5},{5,9},{9,... | collective-permute-start | bytes 491528 | tf_op jit(solution)/shard_map/ppermute | solution.py:18
  12.1 23.8 %collective-permute-start.1 = (bf16[1,2,128,320]{2,3,1,0:T(8,128)(2,1)}, bf16[1,2,128,320]{2,3,1,0:T(8,128)(2,1)}, u32[]{:S(2)}, u32[]{:S(2)}) collective-permute-start(bf16[1,2,128,320]{2,3,1,0:T(8,128)(2,1)} %get-tuple-element.75), channel_id=1, source_target_pairs={{4,0},{8,4},{12,8},{16,12},{20,16},{24,20},{28,24},{5,1},{9,5},{13... | collective-permute-start | bytes 491528 | tf_op jit(solution)/shard_map/ppermute | solution.py:20
  14.6 13.9 %copy-start.6 = (bf16[2,2,128,320]{2,3,1,0:T(8,128)(2,1)S(1)}, bf16[2,2,128,320]{2,3,1,0:T(8,128)(2,1)}, u32[]{:S(2)}) copy-start(bf16[2,2,128,320]{2,3,1,0:T(8,128)(2,1)} %param.9) | copy-start | bytes 983044
  20.1 33.7 %all-to-all-start.2 = ((bf16[8,2,5120]{2,1,0:T(2,128)(2,1)}), bf16[8,2,5120]{2,1,0:T(2,128)(2,1)}, u32[]{:S(2)}, u32[]{:S(2)}) async-start(bf16[8,2,5120]{2,1,0:T(2,128)(2,1)} %reshape.238), calls=%async_computation.2 | async-start | bytes 327680 | tf_op jit(solution)/shard_map/all_to_all | solution.py:55
  34.0 7.4 %copy-start.12 = (bf16[3,320,320]{2,1,0:T(8,128)(2,1)S(1)}, bf16[3,320,320]{2,1,0:T(8,128)(2,1)}, u32[]{:S(2)}) copy-start(bf16[3,320,320]{2,1,0:T(8,128)(2,1)} %param.10) | copy-start | bytes 1843204
  44.5 5.2 copy-start.4
  53.8 22.3 %all-to-all-start = ((bf16[8,2,5120]{2,1,0:T(2,128)(2,1)}), bf16[8,2,5120]{2,1,0:T(2,128)(2,1)}, u32[]{:S(2)}, u32[]{:S(2)}) async-start(bf16[8,2,5120]{2,1,0:T(2,128)(2,1)} %reshape.236), calls=%async_computation | async-start | bytes 327680 | tf_op jit(solution)/shard_map/all_to_all | solution.py:55
  58.9 15.7 %copy-start.8 = (bf16[320,1280]{1,0:T(8,128)(2,1)S(1)}, bf16[320,1280]{1,0:T(8,128)(2,1)}, u32[]{:S(2)}) copy-start(bf16[320,1280]{1,0:T(8,128)(2,1)} %param.14) | copy-start | bytes 2457604
  58.9 118.9 %all-reduce.17.cloned.1.call-start = ((), (), s32[]{:S(2)}) async-start(), calls=%async_computation.7 | async-start | bytes 2621440
  77.5 13.2 %copy-start.14 = (bf16[64,1,1,1280]{3,2,1,0:T(2,128)(2,1)}, bf16[64,1,1,1280]{3,2,1,0:T(2,128)(2,1)S(1)}, u32[]{:S(2)}) copy-start(bf16[64,1,1,1280]{3,2,1,0:T(2,128)(2,1)S(1)} %reshape.237) | copy-start | bytes 491524
  98.1 5.3 %copy-start.21 = (bf16[8,32,4,80]{3,2,1,0:T(4,128)(2,1)S(1)}, bf16[8,32,4,80]{3,2,1,0:T(4,128)(2,1)}, u32[]{:S(2)}) copy-start(bf16[8,32,4,80]{3,2,1,0:T(4,128)(2,1)} %reshape.214) | copy-start | bytes 491524
  107.0 6.8 %copy-start.9 = (bf16[320,1280]{1,0:T(8,128)(2,1)S(1)}, bf16[320,1280]{1,0:T(8,128)(2,1)}, u32[]{:S(2)}) copy-start(bf16[320,1280]{1,0:T(8,128)(2,1)} %param.14) | copy-start | bytes 2457604
  121.3 63.4 %copy-start.15 = (bf16[64,1,1,1280]{3,2,1,0:T(2,128)(2,1)S(1)}, bf16[64,1,1,1280]{3,2,1,0:T(2,128)(2,1)}, u32[]{:S(2)}) copy-start(bf16[64,1,1,1280]{3,2,1,0:T(2,128)(2,1)} %copy-done.14) | copy-start | bytes 491524
  121.3 74.9 %copy-start.10 = (bf16[320,1280]{1,0:T(8,128)(2,1)S(1)}, bf16[320,1280]{1,0:T(8,128)(2,1)}, u32[]{:S(2)}) copy-start(bf16[320,1280]{1,0:T(8,128)(2,1)} %param.11) | copy-start | bytes 2457604
  180.2 11.8 %all-to-all-start.3 = ((bf16[8,1,8,1280]{3,2,1,0:T(8,128)(2,1)}), bf16[8,1,8,1280]{3,2,1,0:T(8,128)(2,1)S(1)}, u32[]{:S(2)}, u32[]{:S(2)}) async-start(bf16[8,1,8,1280]{3,2,1,0:T(8,128)(2,1)} %fusion.43), calls=%async_computation.3 | async-start | bytes 327680 | tf_op jit(solution)/shard_map/all_to_all | solution.py:67
  184.8 12.2 %copy-start.30 = (bf16[2,2,128,320]{2,3,1,0:T(8,128)(2,1)S(1)}, bf16[2,2,128,320]{2,3,1,0:T(8,128)(2,1)}, u32[]{:S(2)}) copy-start(bf16[2,2,128,320]{2,3,1,0:T(8,128)(2,1)} %param.17) | copy-start | bytes 983044
  187.1 10.0 %copy-start.16 = (bf16[3,2,128,320]{2,3,1,0:T(8,128)(2,1)S(1)}, bf16[3,2,128,320]{2,3,1,0:T(8,128)(2,1)}, u32[]{:S(2)}) copy-start(bf16[3,2,128,320]{2,3,1,0:T(8,128)(2,1)} %constant_dynamic-update-slice_fusion.2) | copy-start | bytes 1474564
  192.0 11.2 %all-to-all-start.1 = ((bf16[8,1,8,1280]{3,2,1,0:T(8,128)(2,1)}), bf16[8,1,8,1280]{3,2,1,0:T(8,128)(2,1)}, u32[]{:S(2)}, u32[]{:S(2)}) async-start(bf16[8,1,8,1280]{3,2,1,0:T(8,128)(2,1)} %fusion.42), calls=%async_computation.1 | async-start | bytes 327680 | tf_op jit(solution)/shard_map/all_to_all | solution.py:67
  196.0 121.3 %all-reduce.13.cloned.1.call-start = ((), (), s32[]{:S(2)}) async-start(), calls=%async_computation.5 | async-start | bytes 9502720 | tf_op jit(solution)/shard_map/psum | solution.py:161
  205.7 196.5 %all-reduce.15.cloned.1.call-start = ((), (), s32[]{:S(2)}) async-start(), calls=%async_computation.6 | async-start | bytes 6553600 | tf_op jit(solution)/shard_map/psum | solution.py:157
  211.2 301.0 %all-reduce.11.cloned.1.call-start = ((), (), s32[]{:S(2)}) async-start(), calls=%async_computation.4 | async-start | bytes 9502720 | tf_op jit(solution)/shard_map/psum | solution.py:160
  320.0 87.8 %collective-permute-start.3 = (bf16[1,2,128,320]{2,3,1,0:T(8,128)(2,1)S(1)}, bf16[1,2,128,320]{2,3,1,0:T(8,128)(2,1)S(1)}, u32[]{:S(2)}, u32[]{:S(2)}) collective-permute-start(bf16[1,2,128,320]{2,3,1,0:T(8,128)(2,1)S(1)} %get-tuple-element.73), channel_id=1, source_target_pairs={{0,4},{4,8},{8,12},{12,16},{16,20},{20,24},{24,28},{1,5},{5,9},{9,... | collective-permute-start | bytes 491528 | tf_op jit(solution)/shard_map/ppermute | solution.py:18
  321.6 86.3 %collective-permute-start.2 = (bf16[1,2,128,320]{2,3,1,0:T(8,128)(2,1)S(1)}, bf16[1,2,128,320]{2,3,1,0:T(8,128)(2,1)S(1)}, u32[]{:S(2)}, u32[]{:S(2)}) collective-permute-start(bf16[1,2,128,320]{2,3,1,0:T(8,128)(2,1)S(1)} %get-tuple-element.74), channel_id=1, source_target_pairs={{4,0},{8,4},{12,8},{16,12},{20,16},{24,20},{28,24},{5,1},{9,5},{13... | collective-permute-start | bytes 491528 | tf_op jit(solution)/shard_map/ppermute | solution.py:20
  (31 other events, 62.7 us)
Sparse Core Ops, SparseCore 0:
  121.5 56.2 all-reduce.16
  205.8 111.3 all-reduce.12
  320.3 81.9 all-reduce.14
  404.7 107.4 all-reduce.10
